TPU v7x, 32 devices: a whole 2x2x4 slice. The times are simulated.
32 devices in a mesh: dp: 8 (over z, x), mp: 4 (over y, core).
Axes of the slice: x: 2, y: 2, z: 4, core: 2. Of those that a mesh axis runs over, the one named last changes fastest.
Arguments:
- rows: float32 [16384, 1280], P(('dp', 'mp')), may hold values from -6 to 6
- lengths: int32 [256], P('dp'), may hold values from 1 to 64, as said below
- freq_class: int32 [256], P(('dp', 'mp')), may hold values from 0 to 2
- freq_table: float32 [3, 1280], replicated, may hold values from -3 to 3
- gain_attn: float32 [1280], replicated, may hold values from 0.5 to 1.5
- gain_mlp: float32 [1280], replicated, may hold values from 0.5 to 1.5
- w_qkv: float32 [3, 1280, 1280], P(None, None, 'mp'), may hold values from -0.15625 to 0.15625
- w_out: float32 [1280, 1280], P('mp'), may hold values from -0.5 to 0.5
- w_gate_up: float32 [2, 1280, 5120], P(None, None, 'mp'), may hold values from -0.15625 to 0.15625
- w_down: float32 [5120, 1280], P('mp'), may hold values from -0.15625 to 0.15625
- cotangent: float32 [16384, 1280], P(('dp', 'mp')), may hold values from -6 to 6
Outputs:
- output: float32 [16384, 1280], P(('dp', 'mp'))
- grad_rows: float32 [16384, 1280], P(('dp', 'mp'))
- grad_qkv: float32 [3, 1280, 1280], P(None, None, 'mp')
- grad_out: float32 [1280, 1280], P('mp')
- grad_gate_up: float32 [2, 1280, 5120], P(None, None, 'mp')
- grad_down: float32 [5120, 1280], P('mp')
- grad_gain_attn: float32 [1280], replicated
- grad_gain_mlp: float32 [1280], replicated
- grad_table: float32 [3, 1280], replicated
Inputs may be any that keep to these rules, and one draw needn't show every extreme that they name: `lengths`: the valid patches of a series are the last of its 64 slots; some series has all 64, and some only one.
All inputs are finite; a program needn't handle non-finite values.
Results may differ from a plain program's by a relative error of at most 0.02.
Values may be sent and summed in bfloat16 or wider, within the bound.
A program may use at most 256 MiB of HBM per device.

v0:
```python
import jax
import jax.numpy as jnp
from jax import lax
from jax.sharding import PartitionSpec as P

HS = 80
NFREQ = 3
SEQ = 64
EPSILON = 1e-06
NEGATIVE = -1e30
HIGHEST = lax.Precision.HIGHEST


def rotate(values, cosines, sines):
    half_width = values.shape[-1] // 2
    first_half = values[..., :half_width]
    second_half = values[..., half_width:]
    return jnp.concatenate(
        [first_half * cosines - second_half * sines, second_half * cosines + first_half * sines], -1
    )


def series_tables(series_lengths):
    places = jnp.arange(SEQ, dtype=jnp.int32)
    starts = SEQ - series_lengths
    valid_mask = places[None, :] >= starts[:, None]
    positions = (places[None, :] - starts[:, None]).astype(jnp.float32)
    frequency = 10000.0 ** (-2.0 * jnp.arange(HS // 2, dtype=jnp.float32) / HS)
    angles = positions[:, :, None] * frequency[None, None, :]
    return (valid_mask, jnp.cos(angles)[:, :, None, :], jnp.sin(angles)[:, :, None, :])


def allowed_pairs(valid_mask):
    places = jnp.arange(SEQ, dtype=jnp.int32)
    causal = places[:, None] >= places[None, :]
    itself = places[:, None] == places[None, :]
    return causal[None, None] & (valid_mask[:, None, None, :] | itself[None, None])


def norm_forward(values, gain):
    inverse = lax.rsqrt(jnp.mean(values * values, -1, keepdims=True) + EPSILON)
    return ((values * inverse * gain).astype(jnp.bfloat16), inverse)


def norm_backward(values, inverse, gain, grad_normed):
    normal = values * inverse
    grad_gain = jnp.sum(grad_normed * normal, 0)
    scaled = grad_normed * gain
    grad_values = inverse * (scaled - normal * jnp.mean(scaled * normal, -1, keepdims=True))
    return (grad_values, grad_gain)


def attention_scores(queries, keys, allowed):
    raw_scores = jnp.einsum("sihe,sjhe->shij", queries, keys, preferred_element_type=jnp.float32)
    return jnp.where(allowed, raw_scores * HS ** (-0.5), NEGATIVE)


def body(
    rows,
    lengths,
    freq_class,
    freq_table,
    gain_attn,
    gain_mlp,
    w_qkv,
    w_out,
    w_gate_up,
    w_down,
    cotangent,
):
    local_rows = rows.shape[0]
    mp_index = lax.axis_index("mp")
    series_count = lengths.shape[0]
    group_rows = series_count * SEQ
    heads_width = w_out.shape[0]
    head_count = heads_width // HS
    valid_mask, cosines, sines = series_tables(lengths)
    allowed = allowed_pairs(valid_mask)
    flat_valid = valid_mask.reshape(group_rows).astype(jnp.float32)
    mine_valid = lax.dynamic_slice_in_dim(flat_valid, mp_index * local_rows, local_rows)[:, None]
    classes = jnp.repeat(freq_class, SEQ)
    onehot = (classes[:, None] == jnp.arange(NFREQ, dtype=jnp.int32)[None, :]).astype(jnp.float32)
    start_rows = rows + jnp.dot(onehot, freq_table, precision=HIGHEST)
    normed_mine, inverse_attn = norm_forward(start_rows, gain_attn)
    normed = lax.all_gather(normed_mine, "mp", axis=0, tiled=True)
    qkv_low = w_qkv.astype(jnp.bfloat16)
    projected = jnp.einsum("td,cdf->ctf", normed, qkv_low, preferred_element_type=jnp.float32)
    projected = projected.reshape(3, series_count, SEQ, head_count, HS)
    queries = rotate(projected[0], cosines, sines).astype(jnp.bfloat16)
    keys = rotate(projected[1], cosines, sines).astype(jnp.bfloat16)
    values = projected[2].astype(jnp.bfloat16)
    scores = attention_scores(queries, keys, allowed)
    row_max = jnp.max(scores, -1, keepdims=True)
    exponent = jnp.exp(scores - row_max)
    row_total = jnp.sum(exponent, -1, keepdims=True)
    log_total = row_max + jnp.log(row_total)
    attention = (exponent / row_total).astype(jnp.bfloat16)
    mixed = jnp.einsum("shij,sjhe->sihe", attention, values, preferred_element_type=jnp.float32)
    mixed = mixed.reshape(group_rows, heads_width).astype(jnp.bfloat16)
    out_low = w_out.astype(jnp.bfloat16)
    attn_part = jnp.dot(mixed, out_low, preferred_element_type=jnp.float32)
    after_attn = start_rows + lax.psum_scatter(
        attn_part.astype(jnp.bfloat16), "mp", scatter_dimension=0, tiled=True
    ).astype(jnp.float32)
    normed_mlp_mine, inverse_mlp = norm_forward(after_attn, gain_mlp)
    normed_mlp = lax.all_gather(normed_mlp_mine, "mp", axis=0, tiled=True)
    gate_up_low = w_gate_up.astype(jnp.bfloat16)
    gate_up = jnp.einsum("td,cdf->ctf", normed_mlp, gate_up_low, preferred_element_type=jnp.float32)
    gate_pre = gate_up[0]
    up_pre = gate_up[1]
    sigmoid_gate = jax.nn.sigmoid(gate_pre)
    activated = gate_pre * sigmoid_gate
    hidden = (activated * up_pre).astype(jnp.bfloat16)
    down_low = w_down.astype(jnp.bfloat16)
    mlp_part = jnp.dot(hidden, down_low, preferred_element_type=jnp.float32)
    output = after_attn + lax.psum_scatter(
        mlp_part.astype(jnp.bfloat16), "mp", scatter_dimension=0, tiled=True
    ).astype(jnp.float32)
    grad_output = cotangent * mine_valid
    grad_down_in = lax.all_gather(grad_output.astype(jnp.bfloat16), "mp", axis=0, tiled=True)
    grad_down = jnp.einsum("tf,td->fd", hidden, grad_down_in, preferred_element_type=jnp.float32)
    grad_hidden = jnp.einsum(
        "td,fd->tf", grad_down_in, down_low, preferred_element_type=jnp.float32
    )
    grad_gate = grad_hidden * up_pre * (sigmoid_gate * (1.0 + gate_pre * (1.0 - sigmoid_gate)))
    grad_up = grad_hidden * activated
    grad_pre = jnp.stack([grad_gate, grad_up]).astype(jnp.bfloat16)
    grad_gate_up = jnp.einsum(
        "td,ctf->cdf", normed_mlp, grad_pre, preferred_element_type=jnp.float32
    )
    mlp_back_part = jnp.einsum(
        "ctf,cdf->td", grad_pre, gate_up_low, preferred_element_type=jnp.float32
    )
    grad_normed_mlp = lax.psum_scatter(
        mlp_back_part.astype(jnp.bfloat16), "mp", scatter_dimension=0, tiled=True
    ).astype(jnp.float32)
    grad_rows_mlp, grad_gain_mlp = norm_backward(after_attn, inverse_mlp, gain_mlp, grad_normed_mlp)
    grad_after = grad_output + grad_rows_mlp
    grad_attn_in = lax.all_gather(grad_after.astype(jnp.bfloat16), "mp", axis=0, tiled=True)
    grad_out = jnp.einsum("tf,td->fd", mixed, grad_attn_in, preferred_element_type=jnp.float32)
    grad_mixed = jnp.einsum("td,fd->tf", grad_attn_in, out_low, preferred_element_type=jnp.float32)
    grad_mixed = grad_mixed.astype(jnp.bfloat16).reshape(series_count, SEQ, head_count, HS)
    attention_again = jnp.exp(attention_scores(queries, keys, allowed) - log_total)
    grad_attention = jnp.einsum(
        "sihe,sjhe->shij", grad_mixed, values, preferred_element_type=jnp.float32
    )
    grad_values = jnp.einsum(
        "shij,sihe->sjhe",
        attention_again.astype(jnp.bfloat16),
        grad_mixed,
        preferred_element_type=jnp.float32,
    )
    row_dot = jnp.sum(attention_again * grad_attention, -1, keepdims=True)
    grad_scores = (attention_again * (grad_attention - row_dot)).astype(jnp.bfloat16)
    grad_queries = jnp.einsum(
        "shij,sjhe->sihe", grad_scores, keys, preferred_element_type=jnp.float32
    ) * HS ** (-0.5)
    grad_keys = jnp.einsum(
        "shij,sihe->sjhe", grad_scores, queries, preferred_element_type=jnp.float32
    ) * HS ** (-0.5)
    grad_projected = jnp.stack(
        [rotate(grad_queries, cosines, -sines), rotate(grad_keys, cosines, -sines), grad_values]
    )
    grad_projected = grad_projected.reshape(3, group_rows, heads_width).astype(jnp.bfloat16)
    grad_qkv = jnp.einsum("td,ctf->cdf", normed, grad_projected, preferred_element_type=jnp.float32)
    attn_back_part = jnp.einsum(
        "ctf,cdf->td", grad_projected, qkv_low, preferred_element_type=jnp.float32
    )
    grad_normed = lax.psum_scatter(
        attn_back_part.astype(jnp.bfloat16), "mp", scatter_dimension=0, tiled=True
    ).astype(jnp.float32)
    grad_rows_attn, grad_gain_attn = norm_backward(start_rows, inverse_attn, gain_attn, grad_normed)
    grad_rows = grad_after + grad_rows_attn
    grad_table = jnp.dot(onehot.T, grad_rows, precision=HIGHEST)
    grad_gain_attn, grad_gain_mlp, grad_table, token_total = lax.psum(
        (grad_gain_attn, grad_gain_mlp, grad_table, jnp.sum(mine_valid)), ("dp", "mp")
    )
    grad_qkv, grad_out, grad_gate_up, grad_down = (
        lax.psum(grad_qkv.astype(jnp.bfloat16), "dp").astype(jnp.float32),
        lax.psum(grad_out.astype(jnp.bfloat16), "dp").astype(jnp.float32),
        lax.psum(grad_gate_up.astype(jnp.bfloat16), "dp").astype(jnp.float32),
        lax.psum(grad_down.astype(jnp.bfloat16), "dp").astype(jnp.float32),
    )
    root_scale = lax.rsqrt(token_total)
    return (
        output,
        grad_rows,
        grad_qkv * root_scale,
        grad_out * root_scale,
        grad_gate_up * root_scale,
        grad_down * root_scale,
        grad_gain_attn * root_scale,
        grad_gain_mlp * root_scale,
        grad_table * root_scale,
    )


def solution(mesh):
    return jax.shard_map(
        body,
        mesh=mesh,
        in_specs=(
            P(("dp", "mp"), None),
            P("dp"),
            P(("dp", "mp")),
            P(),
            P(),
            P(),
            P(None, None, "mp"),
            P("mp", None),
            P(None, None, "mp"),
            P("mp", None),
            P(("dp", "mp"), None),
        ),
        out_specs=(
            P(("dp", "mp"), None),
            P(("dp", "mp"), None),
            P(None, None, "mp"),
            P("mp", None),
            P(None, None, "mp"),
            P("mp", None),
            P(),
            P(),
            P(),
        ),
        check_vma=False,
    )
```

profile of v0, /device:TPU:0, one launch (start us, length us, event | category | flops | bytes accessed | tf_op | source)
XLA Modules:
  0.0 1067.2 jit_solution(17084121526547978977)
XLA Ops:
  19.4 36.9 %all-gather.5.cloned.1.call-done = bf16[2048,1280]{1,0:T(8,128)(2,1)} async-done(((bf16[512,1280]{1,0:T(8,128)(2,1)}), bf16[2048,1280]{1,0:T(8,128)(2,1)}) %all-gather.5.cloned.1.call-update) | async-done | bytes 5242896 | tf_op jit(solution)/shard_map/all_gather | solution.py:85
  56.3 8.7 fusion.10
  119.9 7.9 subtract_convert_fusion.3
  143.1 7.1 convolution_convert_fusion.2
  150.3 51.5 %reduce-scatter.5.cloned.1.call-done = bf16[512,1280]{1,0:T(8,128)(2,1)} async-done(((bf16[2048,1280]{1,0:T(8,128)(2,1)}), bf16[512,1280]{1,0:T(8,128)(2,1)}) %reduce-scatter.5.cloned.1.call-update) | async-done | bytes 1310736 | tf_op jit(solution)/shard_map/reduce_scatter | solution.py:102
  208.6 38.5 %all-gather.7.cloned.1.call-done = bf16[2048,1280]{1,0:T(8,128)(2,1)} async-done(((bf16[512,1280]{1,0:T(8,128)(2,1)}), bf16[2048,1280]{1,0:T(8,128)(2,1)}) %all-gather.7.cloned.1.call-update) | async-done | bytes 5242896 | tf_op jit(solution)/shard_map/all_gather | solution.py:106
  247.0 22.6 %convolution_bitcast_fusion = f32[2,2048,1280]{2,1,0:T(8,128)} fusion(bf16[2048,1280]{1,0:T(8,128)(2,1)} %all-gather.7.cloned.1.call-done, f32[2,1280,1280]{2,1,0:T(8,128)} %param.19), kind=kOutput, calls=%fused_computation.1 | convolution fusion | flops 13425049600 | bytes 39321600 | tf_op jit(solution)/shard_map/td,cdf->ctf/dot_general | solution.py:108
  269.6 20.0 %all-gather.9.cloned.1.call-done = bf16[2048,1280]{1,0:T(8,128)(2,1)} async-done(((bf16[512,1280]{1,0:T(8,128)(2,1)}), bf16[2048,1280]{1,0:T(8,128)(2,1)}) %all-gather.9.cloned.1.call-update) | async-done | bytes 5242896 | tf_op jit(solution)/shard_map/all_gather | solution.py:120
  289.6 21.7 %fusion.9 = (bf16[1,2048,1280]{2,1,0:T(8,128)(2,1)}, bf16[1,2048,1280]{2,1,0:T(8,128)(2,1)}, bf16[2048,1280]{1,0:T(8,128)(2,1)}) fusion(f32[2,2048,1280]{2,1,0:T(8,128)} %convolution_bitcast_fusion, bf16[2048,1280]{1,0:T(8,128)(2,1)} %all-gather.9.cloned.1.call-done, f32[1280,1280]{1,0:T(8,128)} %param.20), kind=kOutput, calls=%fused_computation.25 | convolution fusion | flops 6751846400 | bytes 48496640 | tf_op jit(solution)/shard_map/td,fd->tf/dot_general | solution.py:122
  311.2 21.7 %bitcast_convert_fusion.1 = bf16[2048,1280]{1,0:T(8,128)(2,1)} fusion(bf16[1,2048,1280]{2,1,0:T(8,128)(2,1)} %get-tuple-element.46, bf16[1,2048,1280]{2,1,0:T(8,128)(2,1)} %get-tuple-element.45, f32[2,1280,1280]{2,1,0:T(8,128)} %param.19), kind=kOutput, calls=%fused_computation.7 | convolution fusion | flops 13432913920 | bytes 28835840 | tf_op jit(solution)/shard_map/ctf,cdf->td/dot_general | solution.py:131
  333.0 12.4 %convolution_convert_fusion.1 = bf16[2048,1280]{1,0:T(8,128)(2,1)} fusion(bf16[2048,1280]{1,0:T(8,128)(2,1)} %get-tuple-element.47, f32[1280,1280]{1,0:T(8,128)} %param.20), kind=kOutput, calls=%fused_computation.14 | convolution fusion | flops 6715146240 | bytes 17039360 | tf_op jit(solution)/shard_map/dot_general | solution.py:115
  345.4 39.1 %reduce-scatter.9.cloned.1.call-done = bf16[512,1280]{1,0:T(8,128)(2,1)} async-done(((bf16[2048,1280]{1,0:T(8,128)(2,1)}), bf16[512,1280]{1,0:T(8,128)(2,1)}) %reduce-scatter.9.cloned.1.call-update) | async-done | bytes 1310736 | tf_op jit(solution)/shard_map/reduce_scatter | solution.py:134
  386.7 51.7 %reduce-scatter.7.cloned.1.call-done = bf16[512,1280]{1,0:T(8,128)(2,1)} async-done(((bf16[2048,1280]{1,0:T(8,128)(2,1)}), bf16[512,1280]{1,0:T(8,128)(2,1)}) %reduce-scatter.7.cloned.1.call-update) | async-done | bytes 1310736 | tf_op jit(solution)/shard_map/reduce_scatter | solution.py:116
  438.4 6.3 fusion.59
  444.8 40.5 %all-gather.11.cloned.1.call-done = bf16[2048,1280]{1,0:T(8,128)(2,1)} async-done(((bf16[512,1280]{1,0:T(8,128)(2,1)}), bf16[2048,1280]{1,0:T(8,128)(2,1)}) %all-gather.11.cloned.1.call-update) | async-done | bytes 5242896 | tf_op jit(solution)/shard_map/all_gather | solution.py:139
  550.5 9.9 bitcast_convert_fusion
  560.5 12.3 %convolution_convert_fusion.3 = bf16[1280,1280]{1,0:T(8,128)(2,1)} fusion(bf16[2048,1280]{1,0:T(8,128)(2,1)} %get-tuple-element.47, bf16[2048,1280]{1,0:T(8,128)(2,1)} %all-gather.9.cloned.1.call-done), kind=kOutput, calls=%fused_computation.16 | convolution fusion | flops 6712524800 | bytes 13762560 | tf_op jit(solution)/shard_map/tf,td->fd/dot_general | solution.py:121
  572.8 20.2 %fusion.1 = bf16[2,1280,1280]{1,2,0:T(8,128)(2,1)} fusion(bf16[1,2048,1280]{2,1,0:T(8,128)(2,1)} %get-tuple-element.46, bf16[1,2048,1280]{2,1,0:T(8,128)(2,1)} %get-tuple-element.45, bf16[2048,1280]{1,0:T(8,128)(2,1)} %all-gather.7.cloned.1.call-done), kind=kOutput, calls=%fused_computation.13 | convolution fusion | flops 13430292480 | bytes 22282240 | tf_op jit(solution)/shard_map/td,ctf->cdf/dot_general | solution.py:128
  595.9 6.5 fusion.20
  602.5 9.5 reduce-scatter.11.cloned.1.call-done
  617.7 44.2 %all-reduce = (f32[]{:T(128)}, f32[1280]{0:T(1024)S(1)}, f32[1280]{0:T(1024)S(1)}, f32[3,1280]{1,0:T(4,128)S(1)}) all-reduce(f32[]{:T(128)} %get-tuple-element.39, f32[1280]{0:T(1024)S(1)} %get-tuple-element.29, f32[1280]{0:T(1024)S(1)} %get-tuple-element.27, f32[3,1280]{1,0:T(4,128)S(1)} %fusion.49), channel_id=1, replica_groups=mesh['dp'=8,'mp'=4] {'dp','mp'}, use_global_device_ids=true, to_apply=%region_13.14 | all-reduce | flops 6401 | bytes 51208 | tf_op jit(solution)/shard_map/psum | solution.py:175
  664.4 365.7 %all-reduce.4.cloned.1.call-done = (bf16[3,1280,320]{1,2,0:T(8,128)(2,1)}, bf16[320,1280]{1,0:T(8,128)(2,1)}, bf16[2,1280,1280]{1,2,0:T(8,128)(2,1)}, bf16[1280,1280]{1,0:T(8,128)(2,1)}) async-done(((bf16[3,1280,320]{1,2,0:T(8,128)(2,1)}, bf16[320,1280]{1,0:T(8,128)(2,1)}, bf16[2,1280,1280]{1,2,0:T(8,128)(2,1)}, bf16[1280,1280]{1,0:T(8,128)(2,1)}), (bf16[3,1280,320]{1,2,0:T(8,128)(2,1)}, ...) | async-done | bytes 13107216 | tf_op jit(solution)/shard_map/psum | solution.py:179
  1040.7 5.8 convert_multiply_fusion
  1046.5 13.9 %copy.54 = f32[2,1280,1280]{2,1,0:T(8,128)} copy(f32[2,1280,1280]{1,2,0:T(8,128)} %convert_multiply_fusion) | data formatting | bytes 26214400
  (178 shorter events, 177.3 us)
Async XLA Ops:
  7.2 49.1 %all-gather.5.cloned.1.call-start = ((), (), s32[]{:S(2)}) async-start(), calls=%async_computation.4 | async-start | bytes 6553600 | tf_op jit(solution)/shard_map/all_gather | solution.py:85
  8.1 4.9 copy-start.35
  11.3 190.5 %copy-start.4 = (f32[512,1280]{1,0:T(8,128)}, f32[512,1280]{1,0:T(8,128)S(1)}, u32[]{:S(2)}) copy-start(f32[512,1280]{1,0:T(8,128)S(1)} %get-tuple-element.73) | copy-start | bytes 7864324
  13.0 188.8 %reduce-scatter.5.cloned.1.call-start = ((), (), s32[]{:S(2)}) async-start(), calls=%async_computation.5 | async-start | bytes 6553600 | tf_op jit(solution)/shard_map/reduce_scatter | solution.py:102
  150.2 54.8 %copy-start.30 = (f32[1280]{0:T(1024)S(1)}, f32[1280]{0:T(1024)}, u32[]{:S(2)}) copy-start(f32[1280]{0:T(1024)} %param.16) | copy-start | bytes 15364
  150.2 96.8 %all-gather.7.cloned.1.call-start = ((), (), s32[]{:S(2)}) async-start(), calls=%async_computation.6 | async-start | bytes 6553600 | tf_op jit(solution)/shard_map/all_gather | solution.py:106
  206.4 83.1 %all-gather.9.cloned.1.call-start = ((), (), s32[]{:S(2)}) async-start(), calls=%async_computation.8 | async-start | bytes 6553600 | tf_op jit(solution)/shard_map/all_gather | solution.py:120
  208.5 176.0 %reduce-scatter.9.cloned.1.call-start = ((), (), s32[]{:S(2)}) async-start(), calls=%async_computation.9 | async-start | bytes 6553600 | tf_op jit(solution)/shard_map/reduce_scatter | solution.py:134
  333.0 105.4 %reduce-scatter.7.cloned.1.call-start = ((), (), s32[]{:S(2)}) async-start(), calls=%async_computation.7 | async-start | bytes 6553600 | tf_op jit(solution)/shard_map/reduce_scatter | solution.py:116
  345.4 39.1 %copy-start.7 = (f32[512,1280]{1,0:T(8,128)S(1)}, f32[512,1280]{1,0:T(8,128)}, u32[]{:S(2)}) copy-start(f32[512,1280]{1,0:T(8,128)} %copy-done.6) | copy-start | bytes 7864324
  345.4 139.9 %all-gather.11.cloned.1.call-start = ((), (), s32[]{:S(2)}) async-start(), calls=%async_computation.10 | async-start | bytes 6553600 | tf_op jit(solution)/shard_map/all_gather | solution.py:139
  444.7 167.3 %reduce-scatter.11.cloned.1.call-start = ((), (), s32[]{:S(2)}) async-start(), calls=%async_computation.11 | async-start | bytes 6553600 | tf_op jit(solution)/shard_map/reduce_scatter | solution.py:169
  560.4 469.8 %all-reduce.4.cloned.1.call-start = ((), (), s32[]{:S(2)}) async-start(), calls=%async_computation.12 | async-start | bytes 26214400 | tf_op jit(solution)/shard_map/psum | solution.py:179
  560.4 32.6 %slice-start.4 = ((s8[5242880]{0:T(1024)(128)(4,1)}), s8[4194304]{0:T(1024)(128)(4,1)S(1)}, s32[]{:S(2)}) async-start(s8[5242880]{0:T(1024)(128)(4,1)} %bitcast.110), calls=%async_computation.17 | async-start | bytes 8388608
  560.5 35.5 %slice-start.2 = ((s8[5242880]{0:T(1024)(128)(4,1)}), s8[4194304]{0:T(1024)(128)(4,1)S(1)}, s32[]{:S(2)}) async-start(s8[5242880]{0:T(1024)(128)(4,1)} %bitcast.108), calls=%async_computation.15 | async-start | bytes 8388608
  572.8 20.3 %copy-start.27 = (bf16[2048,320]{1,0:T(8,128)(2,1)S(1)}, bf16[2048,320]{1,0:T(8,128)(2,1)}, u32[]{:S(2)}) copy-start(bf16[2048,320]{1,0:T(8,128)(2,1)} %convert_element_type.131) | copy-start | bytes 3932164
  572.8 20.3 %slice-start.5 = ((s8[5242880]{0:T(1024)(128)(4,1)}), s8[1048576]{0:T(1024)(128)(4,1)S(1)}, s32[]{:S(2)}) async-start(s8[5242880]{0:T(1024)(128)(4,1)} %bitcast.110), calls=%async_computation.18 | async-start | bytes 2097152
  572.8 23.1 %slice-start.3 = ((s8[5242880]{0:T(1024)(128)(4,1)}), s8[1048576]{0:T(1024)(128)(4,1)S(1)}, s32[]{:S(2)}) async-start(s8[5242880]{0:T(1024)(128)(4,1)} %bitcast.108), calls=%async_computation.16 | async-start | bytes 2097152
  602.5 9.5 copy-start.5
  602.5 9.5 copy-start.32
  602.5 9.5 copy-start.34
  1032.7 7.0 slice-start
  1036.0 4.7 slice-start.1
  1046.5 13.9 %copy-start.1 = (f32[3,1280]{1,0:T(4,128)S(1)}, f32[3,1280]{1,0:T(4,128)}, u32[]{:S(2)}) copy-start(f32[3,1280]{1,0:T(4,128)} %param.14) | copy-start | bytes 46084
  (29 other events, 76.4 us)
Sparse Core Ops, SparseCore 0:
  13.1 43.1 all-gather.4
  150.3 51.3 reduce-scatter.4
  206.5 40.4 all-gather.6
  249.1 40.4 all-gather.8
  333.1 51.3 reduce-scatter.8
  386.9 51.3 reduce-scatter.6
  444.8 40.4 all-gather.10
  560.5 51.3 reduce-scatter.10
  617.3 412.7 all-reduce.3
where the time goes:
time: 1080 us; the launch traced here: 1070 us
  waiting for transfers between devices  653 us (60%)
  matrix products  168 us (16%)
  local copies, waits for them, and re-layouts  122 us (11%)
  other arithmetic  63.7 us (6%)
  blocking collectives  44.2 us (4%)
  between operations  15.3 us (1%)
    psum x1, waiting for transfers between devices, body(): lax.psum(grad_qkv.astype(jnp.bfloat16), 'dp').astype(jnp.float32)  366 us
    reduce_scatter x1, waiting for transfers between devices, body(): lax.psum_scatter(mlp_part.astype(jnp.bfloat16), 'mp', scatter_dimension=0...  51.7 us
    reduce_scatter x1, waiting for transfers between devices, body(): lax.psum_scatter(attn_part.astype(jnp.bfloat16), 'mp', scatter_dimension=...  51.5 us
    unnamed x95, local copies, waits for them, and re-layouts  46.5 us
    psum x1, blocking collectives, body(): lax.psum((grad_gain_attn, grad_gain_mlp, grad_table, jnp.sum(mine_valid))...  44.2 us
    all_gather x1, waiting for transfers between devices, body(): lax.all_gather(grad_after.astype(jnp.bfloat16), 'mp', axis=0, tiled=True)  40.5 us
    reduce_scatter x1, waiting for transfers between devices, body(): lax.psum_scatter(mlp_back_part.astype(jnp.bfloat16), 'mp', scatter_dimens...  39.1 us
    all_gather x1, waiting for transfers between devices, body(): normed_mlp = lax.all_gather(normed_mlp_mine, 'mp', axis=0, tiled=True)  38.5 us
  transfers between devices with their start and end apart: 9, of which 9 were waited for; matrix products, arithmetic and copies ran while one was open for 9% of the time, Pallas kernels for 0%

commit v1 on v0

--- a/solution.py
+++ b/solution.py
@@ -9,6 +9,17 @@
 EPSILON = 1e-06
 NEGATIVE = -1e30
 HIGHEST = lax.Precision.HIGHEST
+
+
+def pass_along(shard, name, along):
+    peers = lax.axis_size(name)
+    route = [(i, (i + 1) % peers) for i in range(peers)]
+    parts = [shard]
+    for stride in range(1, peers):
+        parts = [lax.ppermute(parts[0], name, route), *parts]
+    whole = jnp.concatenate(parts, axis=along)
+    shift = (lax.axis_index(name) + 1) * parts[-1].shape[along]
+    return jnp.roll(whole, shift, axis=along)
 
 
 def rotate(values, cosines, sines):
@@ -82,7 +93,7 @@
     onehot = (classes[:, None] == jnp.arange(NFREQ, dtype=jnp.int32)[None, :]).astype(jnp.float32)
     start_rows = rows + jnp.dot(onehot, freq_table, precision=HIGHEST)
     normed_mine, inverse_attn = norm_forward(start_rows, gain_attn)
-    normed = lax.all_gather(normed_mine, "mp", axis=0, tiled=True)
+    normed = pass_along(normed_mine, "mp", 0)
     qkv_low = w_qkv.astype(jnp.bfloat16)
     projected = jnp.einsum("td,cdf->ctf", normed, qkv_low, preferred_element_type=jnp.float32)
     projected = projected.reshape(3, series_count, SEQ, head_count, HS)

time: 1080 us -> 1090 us (level)
  waiting for transfers between devices: 653 us -> 664 us
    ppermute x0 -> x3, waiting for transfers between devices: none -> 45.4 us  [pass_along(): parts = [lax.ppermute(parts[0], name, route), *parts]]
    all_gather x1 -> x0, waiting for transfers between devices: 36.9 us -> none  [body(): normed = lax.all_gather(normed_mine, 'mp', axis=0, tiled=True)]
    unnamed x95 -> x109, local copies, waits for them, and re-layouts: 46.5 us -> 52.8 us
  transfers between devices with their start and end apart: 9 -> 11, of which waited for: 9 -> 11; matrix products, arithmetic and copies ran while one was open for 9% -> 9% of each run, Pallas kernels for 0% -> 0%
where the time goes in v1:
time: 1090 us; the launch traced here: 1080 us
  waiting for transfers between devices  664 us (61%)
  matrix products  165 us (15%)
  local copies, waits for them, and re-layouts  128 us (12%)
  other arithmetic  63.3 us (6%)
  blocking collectives  44.2 us (4%)
  between operations  15.7 us (1%)
    psum x1, waiting for transfers between devices, body(): lax.psum(grad_qkv.astype(jnp.bfloat16), 'dp').astype(jnp.float32)  366 us
    reduce_scatter x1, waiting for transfers between devices, body(): lax.psum_scatter(attn_part.astype(jnp.bfloat16), 'mp', scatter_dimension=...  53.5 us
    unnamed x109, local copies, waits for them, and re-layouts  52.8 us
    reduce_scatter x1, waiting for transfers between devices, body(): lax.psum_scatter(mlp_part.astype(jnp.bfloat16), 'mp', scatter_dimension=0...  51.7 us
    ppermute x3, waiting for transfers between devices, pass_along(): parts = [lax.ppermute(parts[0], name, route), *parts]  45.4 us
    psum x1, blocking collectives, body(): lax.psum((grad_gain_attn, grad_gain_mlp, grad_table, jnp.sum(mine_valid))...  44.2 us
    all_gather x1, waiting for transfers between devices, body(): lax.all_gather(grad_after.astype(jnp.bfloat16), 'mp', axis=0, tiled=True)  40.5 us
    reduce_scatter x1, waiting for transfers between devices, body(): lax.psum_scatter(mlp_back_part.astype(jnp.bfloat16), 'mp', scatter_dimens...  39.1 us
  transfers between devices with their start and end apart: 11, of which 11 were waited for; matrix products, arithmetic and copies ran while one was open for 9% of the time, Pallas kernels for 0%

profile of v1, /device:TPU:0, one launch (start us, length us, event | category | flops | bytes accessed | tf_op | source)
XLA Modules:
  0.0 1081.1 jit_solution(8714242570282082349)
XLA Ops:
  12.1 17.4 %collective-permute-done = bf16[512,1280]{1,0:T(8,128)(2,1)} collective-permute-done((bf16[512,1280]{1,0:T(8,128)(2,1)S(1)}, bf16[512,1280]{1,0:T(8,128)(2,1)}, u32[]{:S(2)}, u32[]{:S(2)}) %collective-permute-start) | collective-permute-done | bytes 1310752 | tf_op jit(solution)/shard_map/ppermute | solution.py:19
  29.5 17.3 %collective-permute-done.1 = bf16[512,1280]{1,0:T(8,128)(2,1)} collective-permute-done((bf16[512,1280]{1,0:T(8,128)(2,1)}, bf16[512,1280]{1,0:T(8,128)(2,1)}, u32[]{:S(2)}, u32[]{:S(2)}) %collective-permute-start.1) | collective-permute-done | bytes 1310752 | tf_op jit(solution)/shard_map/ppermute | solution.py:19
  53.3 10.8 collective-permute-done.2
  131.1 8.1 subtract_convert_fusion.3
  154.4 7.1 convolution_convert_fusion.2
  161.6 53.5 %reduce-scatter.5.cloned.1.call-done = bf16[512,1280]{1,0:T(8,128)(2,1)} async-done(((bf16[2048,1280]{1,0:T(8,128)(2,1)}), bf16[512,1280]{1,0:T(8,128)(2,1)}) %reduce-scatter.5.cloned.1.call-update) | async-done | bytes 1310736 | tf_op jit(solution)/shard_map/reduce_scatter | solution.py:113
  221.9 38.4 %all-gather.4.cloned.1.call-done = bf16[2048,1280]{1,0:T(8,128)(2,1)} async-done(((bf16[512,1280]{1,0:T(8,128)(2,1)}), bf16[2048,1280]{1,0:T(8,128)(2,1)}) %all-gather.4.cloned.1.call-update) | async-done | bytes 5242896 | tf_op jit(solution)/shard_map/all_gather | solution.py:117
  260.3 22.8 %convolution_bitcast_fusion = f32[2,2048,1280]{2,1,0:T(8,128)} fusion(bf16[2048,1280]{1,0:T(8,128)(2,1)} %all-gather.4.cloned.1.call-done, f32[2,1280,1280]{2,1,0:T(8,128)} %param.19), kind=kOutput, calls=%fused_computation.1 | convolution fusion | flops 13425049600 | bytes 39321600 | tf_op jit(solution)/shard_map/td,cdf->ctf/dot_general | solution.py:119
  283.1 19.9 %all-gather.6.cloned.1.call-done = bf16[2048,1280]{1,0:T(8,128)(2,1)} async-done(((bf16[512,1280]{1,0:T(8,128)(2,1)}), bf16[2048,1280]{1,0:T(8,128)(2,1)}) %all-gather.6.cloned.1.call-update) | async-done | bytes 5242896 | tf_op jit(solution)/shard_map/all_gather | solution.py:131
  303.0 21.7 %fusion.9 = (bf16[1,2048,1280]{2,1,0:T(8,128)(2,1)}, bf16[1,2048,1280]{2,1,0:T(8,128)(2,1)}, bf16[2048,1280]{1,0:T(8,128)(2,1)}) fusion(f32[2,2048,1280]{2,1,0:T(8,128)} %convolution_bitcast_fusion, bf16[2048,1280]{1,0:T(8,128)(2,1)} %all-gather.6.cloned.1.call-done, f32[1280,1280]{1,0:T(8,128)} %param.20), kind=kOutput, calls=%fused_computation.25 | convolution fusion | flops 6751846400 | bytes 48496640 | tf_op jit(solution)/shard_map/td,fd->tf/dot_general | solution.py:133
  324.7 21.5 %bitcast_convert_fusion.1 = bf16[2048,1280]{1,0:T(8,128)(2,1)} fusion(bf16[1,2048,1280]{2,1,0:T(8,128)(2,1)} %get-tuple-element.46, bf16[1,2048,1280]{2,1,0:T(8,128)(2,1)} %get-tuple-element.45, f32[2,1280,1280]{2,1,0:T(8,128)} %param.19), kind=kOutput, calls=%fused_computation.7 | convolution fusion | flops 13432913920 | bytes 28835840 | tf_op jit(solution)/shard_map/ctf,cdf->td/dot_general | solution.py:142
  346.3 12.4 %convolution_convert_fusion.1 = bf16[2048,1280]{1,0:T(8,128)(2,1)} fusion(bf16[2048,1280]{1,0:T(8,128)(2,1)} %get-tuple-element.47, f32[1280,1280]{1,0:T(8,128)} %param.20), kind=kOutput, calls=%fused_computation.14 | convolution fusion | flops 6715146240 | bytes 17039360 | tf_op jit(solution)/shard_map/dot_general | solution.py:126
  358.7 39.1 %reduce-scatter.9.cloned.1.call-done = bf16[512,1280]{1,0:T(8,128)(2,1)} async-done(((bf16[2048,1280]{1,0:T(8,128)(2,1)}), bf16[512,1280]{1,0:T(8,128)(2,1)}) %reduce-scatter.9.cloned.1.call-update) | async-done | bytes 1310736 | tf_op jit(solution)/shard_map/reduce_scatter | solution.py:145
  399.9 51.7 %reduce-scatter.7.cloned.1.call-done = bf16[512,1280]{1,0:T(8,128)(2,1)} async-done(((bf16[2048,1280]{1,0:T(8,128)(2,1)}), bf16[512,1280]{1,0:T(8,128)(2,1)}) %reduce-scatter.7.cloned.1.call-update) | async-done | bytes 1310736 | tf_op jit(solution)/shard_map/reduce_scatter | solution.py:127
  451.6 6.3 fusion.63
  458.0 40.5 %all-gather.8.cloned.1.call-done = bf16[2048,1280]{1,0:T(8,128)(2,1)} async-done(((bf16[512,1280]{1,0:T(8,128)(2,1)}), bf16[2048,1280]{1,0:T(8,128)(2,1)}) %all-gather.8.cloned.1.call-update) | async-done | bytes 5242896 | tf_op jit(solution)/shard_map/all_gather | solution.py:150
  564.0 9.9 bitcast_convert_fusion
  574.0 12.0 %convolution_convert_fusion.3 = bf16[1280,1280]{1,0:T(8,128)(2,1)} fusion(bf16[2048,1280]{1,0:T(8,128)(2,1)} %get-tuple-element.47, bf16[2048,1280]{1,0:T(8,128)(2,1)} %all-gather.6.cloned.1.call-done), kind=kOutput, calls=%fused_computation.16 | convolution fusion | flops 6712524800 | bytes 13762560 | tf_op jit(solution)/shard_map/tf,td->fd/dot_general | solution.py:132
  586.1 20.3 %fusion.1 = bf16[2,1280,1280]{1,2,0:T(8,128)(2,1)} fusion(bf16[1,2048,1280]{2,1,0:T(8,128)(2,1)} %get-tuple-element.46, bf16[1,2048,1280]{2,1,0:T(8,128)(2,1)} %get-tuple-element.45, bf16[2048,1280]{1,0:T(8,128)(2,1)} %all-gather.4.cloned.1.call-done), kind=kOutput, calls=%fused_computation.13 | convolution fusion | flops 13430292480 | bytes 22282240 | tf_op jit(solution)/shard_map/td,ctf->cdf/dot_general | solution.py:139
  609.3 6.5 fusion.22
  615.9 9.7 reduce-scatter.11.cloned.1.call-done
  631.3 44.2 %all-reduce = (f32[]{:T(128)}, f32[1280]{0:T(1024)S(1)}, f32[1280]{0:T(1024)S(1)}, f32[3,1280]{1,0:T(4,128)S(1)}) all-reduce(f32[]{:T(128)} %get-tuple-element.39, f32[1280]{0:T(1024)S(1)} %get-tuple-element.29, f32[1280]{0:T(1024)S(1)} %get-tuple-element.27, f32[3,1280]{1,0:T(4,128)S(1)} %fusion.51), channel_id=1, replica_groups=mesh['dp'=8,'mp'=4] {'dp','mp'}, use_global_device_ids=true, to_apply=%region_13.14 | all-reduce | flops 6401 | bytes 51208 | tf_op jit(solution)/shard_map/psum | solution.py:186
  678.0 365.7 %all-reduce.4.cloned.1.call-done = (bf16[3,1280,320]{1,2,0:T(8,128)(2,1)}, bf16[320,1280]{1,0:T(8,128)(2,1)}, bf16[2,1280,1280]{1,2,0:T(8,128)(2,1)}, bf16[1280,1280]{1,0:T(8,128)(2,1)}) async-done(((bf16[3,1280,320]{1,2,0:T(8,128)(2,1)}, bf16[320,1280]{1,0:T(8,128)(2,1)}, bf16[2,1280,1280]{1,2,0:T(8,128)(2,1)}, bf16[1280,1280]{1,0:T(8,128)(2,1)}), (bf16[3,1280,320]{1,2,0:T(8,128)(2,1)}, ...) | async-done | bytes 13107216 | tf_op jit(solution)/shard_map/psum | solution.py:190
  1060.1 13.9 %copy.54 = f32[2,1280,1280]{2,1,0:T(8,128)} copy(f32[2,1280,1280]{1,2,0:T(8,128)} %convert_multiply_fusion) | data formatting | bytes 26214400
  (198 shorter events, 194.6 us)
Async XLA Ops:
  7.2 207.9 %reduce-scatter.5.cloned.1.call-start = ((), (), s32[]{:S(2)}) async-start(), calls=%async_computation.4 | async-start | bytes 6553600 | tf_op jit(solution)/shard_map/reduce_scatter | solution.py:113
  8.1 38.8 %copy-start.38 = (s32[32]{0:T(128)S(1)}, s32[32]{0:T(128)}, u32[]{:S(2)}) copy-start(s32[32]{0:T(128)} %param.12) | copy-start | bytes 388
  11.3 203.9 %copy-start.2 = (f32[512,1280]{1,0:T(8,128)}, f32[512,1280]{1,0:T(8,128)S(1)}, u32[]{:S(2)}) copy-start(f32[512,1280]{1,0:T(8,128)S(1)} %get-tuple-element.73) | copy-start | bytes 7864324
  11.3 59.1 %copy-start.33 = (f32[512]{0:T(512)}, f32[512]{0:T(512)S(1)}, u32[]{:S(2)}) copy-start(f32[512]{0:T(512)S(1)} %add_rsqrt_fusion.1) | copy-start | bytes 6148
  11.6 17.9 %collective-permute-start = (bf16[512,1280]{1,0:T(8,128)(2,1)S(1)}, bf16[512,1280]{1,0:T(8,128)(2,1)}, u32[]{:S(2)}, u32[]{:S(2)}) collective-permute-start(bf16[512,1280]{1,0:T(8,128)(2,1)S(1)} %multiply_convert_fusion.5), channel_id=1, source_target_pairs={{0,1},{1,2},{2,3},{3,0},{4,5},{5,6},{6,7},{7,4},{8,9},{9,10},{10,1... | collective-permute-start | bytes 3932168 | tf_op jit(solution)/shard_map/ppermute | solution.py:19
  29.5 17.3 %collective-permute-start.1 = (bf16[512,1280]{1,0:T(8,128)(2,1)}, bf16[512,1280]{1,0:T(8,128)(2,1)}, u32[]{:S(2)}, u32[]{:S(2)}) collective-permute-start(bf16[512,1280]{1,0:T(8,128)(2,1)} %collective-permute-done), channel_id=1, source_target_pairs={{0,1},{1,2},{2,3},{3,0},{4,5},{5,6},{6,7},{7,4},{8,9},{9,10},{10,1... | collective-permute-start | bytes 3932168 | tf_op jit(solution)/shard_map/ppermute | solution.py:19
  46.8 17.2 %collective-permute-start.2 = (bf16[512,1280]{1,0:T(8,128)(2,1)}, bf16[512,1280]{1,0:T(8,128)(2,1)S(1)}, u32[]{:S(2)}, u32[]{:S(2)}) collective-permute-start(bf16[512,1280]{1,0:T(8,128)(2,1)} %collective-permute-done.1), channel_id=1, source_target_pairs={{0,1},{1,2},{2,3},{3,0},{4,5},{5,6},{6,7},{7,4},{8,9},{9,10},{10,1... | collective-permute-start | bytes 3932168 | tf_op jit(solution)/shard_map/ppermute | solution.py:19
  161.6 56.8 %copy-start.35 = (f32[1280]{0:T(1024)S(1)}, f32[1280]{0:T(1024)}, u32[]{:S(2)}) copy-start(f32[1280]{0:T(1024)} %param.16) | copy-start | bytes 15364
  161.6 98.8 %all-gather.4.cloned.1.call-start = ((), (), s32[]{:S(2)}) async-start(), calls=%async_computation.5 | async-start | bytes 6553600 | tf_op jit(solution)/shard_map/all_gather | solution.py:117
  219.8 83.3 %all-gather.6.cloned.1.call-start = ((), (), s32[]{:S(2)}) async-start(), calls=%async_computation.7 | async-start | bytes 6553600 | tf_op jit(solution)/shard_map/all_gather | solution.py:131
  221.8 175.9 %reduce-scatter.9.cloned.1.call-start = ((), (), s32[]{:S(2)}) async-start(), calls=%async_computation.8 | async-start | bytes 6553600 | tf_op jit(solution)/shard_map/reduce_scatter | solution.py:145
  346.2 105.4 %reduce-scatter.7.cloned.1.call-start = ((), (), s32[]{:S(2)}) async-start(), calls=%async_computation.6 | async-start | bytes 6553600 | tf_op jit(solution)/shard_map/reduce_scatter | solution.py:127
  358.6 39.1 %copy-start.7 = (f32[512,1280]{1,0:T(8,128)S(1)}, f32[512,1280]{1,0:T(8,128)}, u32[]{:S(2)}) copy-start(f32[512,1280]{1,0:T(8,128)} %copy-done.6) | copy-start | bytes 7864324
  358.7 139.9 %all-gather.8.cloned.1.call-start = ((), (), s32[]{:S(2)}) async-start(), calls=%async_computation.9 | async-start | bytes 6553600 | tf_op jit(solution)/shard_map/all_gather | solution.py:150
  457.9 167.6 %reduce-scatter.11.cloned.1.call-start = ((), (), s32[]{:S(2)}) async-start(), calls=%async_computation.10 | async-start | bytes 6553600 | tf_op jit(solution)/shard_map/reduce_scatter | solution.py:180
  574.0 469.7 %all-reduce.4.cloned.1.call-start = ((), (), s32[]{:S(2)}) async-start(), calls=%async_computation.11 | async-start | bytes 26214400 | tf_op jit(solution)/shard_map/psum | solution.py:190
  574.0 32.4 %slice-start.5 = ((s8[5242880]{0:T(1024)(128)(4,1)}), s8[4194304]{0:T(1024)(128)(4,1)S(1)}, s32[]{:S(2)}) async-start(s8[5242880]{0:T(1024)(128)(4,1)} %bitcast.110), calls=%async_computation.17 | async-start | bytes 8388608
  574.0 35.2 %slice-start.2 = ((s8[10485760]{0:T(1024)(128)(4,1)}), s8[4194304]{0:T(1024)(128)(4,1)S(1)}, s32[]{:S(2)}) async-start(s8[10485760]{0:T(1024)(128)(4,1)} %bitcast.108), calls=%async_computation.14 | async-start | bytes 8388608
  586.1 20.4 %copy-start.27 = (bf16[2048,320]{1,0:T(8,128)(2,1)S(1)}, bf16[2048,320]{1,0:T(8,128)(2,1)}, u32[]{:S(2)}) copy-start(bf16[2048,320]{1,0:T(8,128)(2,1)} %convert_element_type.131) | copy-start | bytes 3932164
  586.1 20.4 %slice-start.6 = ((s8[5242880]{0:T(1024)(128)(4,1)}), s8[1048576]{0:T(1024)(128)(4,1)S(1)}, s32[]{:S(2)}) async-start(s8[5242880]{0:T(1024)(128)(4,1)} %bitcast.110), calls=%async_computation.18 | async-start | bytes 2097152
  586.1 23.2 %slice-start.3 = ((s8[10485760]{0:T(1024)(128)(4,1)}), s8[4194304]{0:T(1024)(128)(4,1)S(1)}, s32[]{:S(2)}) async-start(s8[10485760]{0:T(1024)(128)(4,1)} %bitcast.108), calls=%async_computation.15 | async-start | bytes 8388608
  586.1 23.2 %slice-start.4 = ((s8[10485760]{0:T(1024)(128)(4,1)}), s8[2097152]{0:T(1024)(128)(4,1)S(1)}, s32[]{:S(2)}) async-start(s8[10485760]{0:T(1024)(128)(4,1)} %bitcast.108), calls=%async_computation.16 | async-start | bytes 4194304
  615.8 9.7 copy-start.34
  1060.1 13.9 %copy-start.1 = (f32[3,1280]{1,0:T(4,128)S(1)}, f32[3,1280]{1,0:T(4,128)}, u32[]{:S(2)}) copy-start(f32[3,1280]{1,0:T(4,128)} %param.14) | copy-start | bytes 46084
  (35 other events, 119.3 us)
Sparse Core Ops, SparseCore 0:
  161.7 53.4 reduce-scatter.4
  219.9 40.4 all-gather.3
  262.6 40.4 all-gather.5
  346.3 51.3 reduce-scatter.8
  400.2 51.3 reduce-scatter.6
  458.0 40.4 all-gather.7
  574.1 51.3 reduce-scatter.10
  630.9 412.7 all-reduce.3
